TPU v7x, 32 devices: a whole 2x2x4 slice. The times are simulated.
32 devices in a mesh: tm: 4 (over y, core), lat: 4 (over z), lon: 2 (over x).
Axes of the slice: x: 2, y: 2, z: 4, core: 2. Of those that a mesh axis runs over, the one named last changes fastest.
Arguments:
- state: bfloat16 [4, 4, 137, 32, 512], P('tm', None, None, 'lat', 'lon'), may hold values from -6 to 6
- band_counts: int32 [4, 4], P('tm', 'lat'), may hold values from 2 to 6
- dep_blocks: int32 [4, 32, 4, 6], P('tm', 'lat', 'lon'), may hold values from 0 to 3, as said below
- lon_entry: int32 [4, 32, 512], P('tm', 'lat', 'lon'), may hold values from 0 to 5
- lon_offset: int32 [4, 32, 512], P('tm', 'lat', 'lon'), may hold values from 1 to 125
- lon_frac: float32 [4, 32, 512], P('tm', 'lat', 'lon'), may hold values from 0 to 1
- lat_offset: int32 [4, 32, 512], P('tm', 'lat', 'lon'), may hold values from -1 to 0
- lat_frac: float32 [4, 32, 512], P('tm', 'lat', 'lon'), may hold values from 0 to 1
Outputs:
- misfit: bfloat16 [4, 4, 137, 32, 512], P('tm', None, None, 'lat', 'lon')
Inputs may be any that keep to these rules, and one draw needn't show every extreme that they name: `dep_blocks`: the list of a destination block names each of the 6 blocks of its latitude row that lie from 3 blocks west of the first block of the destination's tile to 1 block east of the tile's last block (block numbers taken modulo 4) exactly once, in an order drawn for each block.
All inputs are finite; a program needn't handle non-finite values.
Results may differ from a plain program's by a relative error of at most 0.0046.
Values may be sent and summed in bfloat16 or wider, within the bound.
A program may use at most 64 MiB of HBM per device.

v0:
```python
import jax
import jax.numpy as jnp
from jax import lax
from jax.sharding import PartitionSpec as P

BLK = 128


def shifted(value, axis, steps):
    count = lax.axis_size(axis)
    pairs = [(source, (source + steps) % count) for source in range(count)]
    return lax.ppermute(value, axis, pairs)


def with_halo(shard, sides, width):
    for axis, dim in sides:
        devices, length = (lax.axis_size(axis), shard.shape[dim])
        up = [(i, (i + 1) % devices) for i in range(devices - 1)]
        down = [(j, i) for i, j in up]
        last = lax.slice_in_dim(shard, length - width, length, axis=dim)
        leading = lax.slice_in_dim(shard, 0, width, axis=dim)
        before = lax.ppermute(last, axis, up)
        after = lax.ppermute(leading, axis, down)
        shard = jnp.concatenate([before, shard, after], axis=dim)
    return shard


def from_behind(block, axis, distance):
    devices = range(lax.axis_size(axis))
    route = [(i - distance, i) for i in devices if i - distance in devices]
    return lax.ppermute(block, axis, route)


def cubic_weights(fraction):
    return jnp.stack(
        [
            -fraction * (fraction - 1.0) * (fraction - 2.0) / 6.0,
            (fraction + 1.0) * (fraction - 1.0) * (fraction - 2.0) / 2.0,
            -(fraction + 1.0) * fraction * (fraction - 2.0) / 2.0,
            (fraction + 1.0) * fraction * (fraction - 1.0) / 6.0,
        ]
    )


def body(state, band_counts, dep_blocks, lon_entry, lon_offset, lon_frac, lat_offset, lat_frac):
    fields_n, levels, lat_rows, lon_cols = state.shape[1:]
    depth_rows = fields_n * levels
    blocks = lon_cols // BLK
    margin = blocks // 2
    flattened = state.reshape(depth_rows, lat_rows, lon_cols)
    western = shifted(flattened, "lon", 1)
    second_west = shifted(flattened, "lon", 2)
    eastern = shifted(flattened, "lon", -1)
    far_part = second_west[:, :, margin * BLK :]
    near_part = eastern[:, :, : margin * BLK]
    source = jnp.concatenate([far_part, western, flattened, near_part], axis=2)
    source = source.reshape(depth_rows, lat_rows, 3 * blocks, BLK)
    spread = blocks + margin
    placed = (dep_blocks[0] - lax.axis_index("lon") * blocks + spread) % (
        blocks * lax.axis_size("lon")
    )
    live_count = band_counts[0, 0]
    entry_slot = (lon_entry[0] % live_count).reshape(lat_rows, blocks, BLK)
    offset = lon_offset[0].reshape(lat_rows, blocks, BLK)
    weights = cubic_weights(lon_frac[0].reshape(lat_rows, blocks, BLK)).astype(jnp.bfloat16)
    within = jnp.arange(BLK, dtype=jnp.int32)[:, None]
    gap_table = within[None, None, :, :] - offset[:, :, None, :]
    candidates = jnp.arange(3 * blocks, dtype=jnp.int32)

    def add_entry(entry_index, accumulated):
        chosen = lax.dynamic_index_in_dim(placed, entry_index, 2, keepdims=False)
        selector = (chosen[:, :, None] == candidates[None, None, :]).astype(jnp.bfloat16)
        upstream = jnp.einsum(
            "frqs,rbq->frbs", source, selector, preferred_element_type=jnp.float32
        ).astype(jnp.bfloat16)
        live = (entry_slot == entry_index)[:, :, None, :]
        matrix = jnp.zeros(gap_table.shape, jnp.bfloat16)
        for stencil_node in range(4):
            matrix = jnp.where(
                (gap_table == stencil_node - 1) & live, weights[stencil_node][:, :, None, :], matrix
            )
        return accumulated + jnp.einsum(
            "frbs,rbsc->frbc", upstream, matrix, preferred_element_type=jnp.float32
        )

    accumulated = lax.fori_loop(
        0, live_count, add_entry, jnp.zeros((depth_rows, lat_rows, blocks, BLK), jnp.float32)
    )
    advected = accumulated.astype(jnp.bfloat16).reshape(depth_rows, lat_rows, lon_cols)
    padded = with_halo(advected, (("lat", 1),), 2)
    lat_weights = cubic_weights(lat_frac[0])
    lat_shift = lat_offset[0]
    end_sum = jnp.zeros((depth_rows, lat_rows, lon_cols), jnp.float32)
    for shift_rows in range(-2, 3):
        coefficient = jnp.zeros((lat_rows, lon_cols), jnp.float32)
        for node_index in range(4):
            coefficient = coefficient + jnp.where(
                lat_shift + node_index - 1 == shift_rows, lat_weights[node_index], 0.0
            )
        end_sum = end_sum + coefficient[None, :, :] * padded[
            :, 2 + shift_rows : 2 + shift_rows + lat_rows, :
        ].astype(jnp.float32)
    end_state = end_sum.astype(jnp.bfloat16)
    previous = from_behind(end_state, "tm", 1)
    misfit = (flattened.astype(jnp.float32) - previous.astype(jnp.float32)).astype(jnp.bfloat16)
    return misfit.reshape(state.shape)


def solution(mesh):
    placed = (
        P("tm", None, None, "lat", "lon"),
        P("tm", "lat"),
        P("tm", "lat", "lon", None),
        P("tm", "lat", "lon"),
        P("tm", "lat", "lon"),
        P("tm", "lat", "lon"),
        P("tm", "lat", "lon"),
        P("tm", "lat", "lon"),
    )
    return jax.shard_map(
        body,
        mesh=mesh,
        in_specs=placed,
        out_specs=P("tm", None, None, "lat", "lon"),
        check_vma=False,
    )
```

profile of v0, /device:TPU:1, one launch (start us, length us, event | category | flops | bytes accessed | tf_op | source)
XLA Modules:
  0.0 201.5 jit_solution(14930348205679614322)
XLA Ops:
  0.0 2.0 %collective-permute-start.1 = (bf16[548,8,256]{2,1,0:T(8,128)(2,1)}, bf16[548,8,256]{2,1,0:T(8,128)(2,1)}, u32[]{:S(2)}, u32[]{:S(2)}) collective-permute-start(bf16[548,8,256]{2,1,0:T(8,128)(2,1)} %bitcast.84), channel_id=1, source_target_pairs={{0,1},{1,0},{2,3},{3,2},{4,5},{5,4},{6,7},{7,6},{8,9},{9,8},{10,11... | collective-permute-start | bytes 6733832 | tf_op jit(solution)/shard_map/ppermute | solution.py:12
  2.0 17.8 %collective-permute-start = (bf16[548,8,256]{2,1,0:T(8,128)(2,1)}, bf16[548,8,256]{2,1,0:T(8,128)(2,1)}, u32[]{:S(2)}, u32[]{:S(2)}) collective-permute-start(bf16[548,8,256]{2,1,0:T(8,128)(2,1)} %bitcast.85), channel_id=1, source_target_pairs={{0,0},{1,1},{2,2},{3,3},{4,4},{5,5},{6,6},{7,7},{8,8},{9,9},{10,10... | collective-permute-start | bytes 6733832 | tf_op jit(solution)/shard_map/ppermute | solution.py:12
  23.5 27.4 %collective-permute-done.1 = bf16[548,8,256]{2,1,0:T(8,128)(2,1)} collective-permute-done((bf16[548,8,256]{2,1,0:T(8,128)(2,1)}, bf16[548,8,256]{2,1,0:T(8,128)(2,1)}, u32[]{:S(2)}, u32[]{:S(2)}) %collective-permute-start.1) | collective-permute-done | bytes 2244640 | tf_op jit(solution)/shard_map/ppermute | solution.py:12
  53.6 5.0 %maximum_bitcast_fusion = bf16[548,8,6,128]{3,1,2,0:T(8,128)(2,1)} fusion(bf16[548,8,128]{2,1,0:T(8,128)(2,1)S(1)} %slice.53, bf16[548,8,256]{2,1,0:T(8,128)(2,1)S(1)} %bitcast.86, bf16[548,8,256]{2,1,0:T(8,128)(2,1)} %collective-permute-done.1, bf16[548,8,128]{2,1,0:T(8,128)(2,1)S(1)} %slice.52), kind=kLoop, calls=%fused_computation.46 | loop fusion | flops 26935296 | bytes 13467648 | tf_op jit(solution)/shard_map/reshape | solution.py:57
  58.5 8.1 %copy.16 = bf16[548,8,6,128]{3,2,0,1:T(8,128)(2,1)} copy(bf16[548,8,6,128]{3,1,2,0:T(8,128)(2,1)} %maximum_bitcast_fusion) | data formatting | bytes 13467648
  66.7 2.5 %broadcast_in_dim.66 = f32[548,8,2,128]{3,0,2,1:T(8,128)} broadcast(f32[]{:T(128)} %constant.78.clone.1), dimensions={} | broadcast | bytes 4489220 | tf_op jit(solution)/shard_map/broadcast_in_dim | solution.py:87
  69.1 64.6 %while.11 = (s32[]{:T(128)}, f32[548,8,2,128]{3,0,2,1:T(8,128)}, s32[]{:T(128)}, s32[8,2,128]{2,1,0:T(2,128)S(1)}, bf16[4,8,2,128]{3,2,1,0:T(2,128)(2,1)S(1)}, /...) while((s32[]{:T(128)}, f32[548,8,2,128]{3,0,2,1:T(8,128)}, ...), condition=%wide.region_1.2_spmd.clone, body=%wide.region_0.1_spmd.clone.sunk | while | flops 306432096 | bytes 20271576 | solution.py:86
  69.9 6.1 %fusion.78 = bf16[548,8,2,128]{3,2,0,1:T(2,128)(2,1)S(1)} fusion(bf16[548,8,6,128]{3,2,0,1:T(8,128)(2,1)} %get-tuple-element.208, s32[8,2]{1,0:T(8,128)S(1)} %copy.30), kind=kOutput, calls=%fused_computation.4.clone.1 | convolution fusion | flops 14590048 | bytes 8978496 | tf_op jit(solution)/shard_map/while/body/frqs,rbq->frbs/dot_general | solution.py:73
  76.0 5.9 %bitcast_add_fusion.4 = f32[548,8,2,128]{3,0,2,1:T(8,128)} fusion(f32[548,8,2,128]{3,0,2,1:T(8,128)} %get-tuple-element.192, bf16[548,8,2,128]{3,2,0,1:T(2,128)(2,1)S(1)} %fusion.78, s32[8,2,128]{2,1,0:T(2,128)S(1)} %get-tuple-element.209, pred[8,2,128]{2,1,0:T(4,128)(4,1)S(1)} %broadcast_compare_fusion.2, ...), kind=kOutput, calls=%fused_computation.2.clone.1 | convolution fusion | flops 291840000 | bytes 11249664 | tf_op jit(solution)/shard_map/while/body/frbs,rbsc->frbc/dot_general | solution.py:82
  82.7 6.1 %fusion.78 = bf16[548,8,2,128]{3,2,0,1:T(2,128)(2,1)S(1)} fusion(bf16[548,8,6,128]{3,2,0,1:T(8,128)(2,1)} %get-tuple-element.208, s32[8,2]{1,0:T(8,128)S(1)} %copy.30), kind=kOutput, calls=%fused_computation.4.clone.1 | convolution fusion | flops 14590048 | bytes 8978496 | tf_op jit(solution)/shard_map/while/body/frqs,rbq->frbs/dot_general | solution.py:73
  88.8 5.9 %bitcast_add_fusion.4 = f32[548,8,2,128]{3,0,2,1:T(8,128)} fusion(f32[548,8,2,128]{3,0,2,1:T(8,128)} %get-tuple-element.192, bf16[548,8,2,128]{3,2,0,1:T(2,128)(2,1)S(1)} %fusion.78, s32[8,2,128]{2,1,0:T(2,128)S(1)} %get-tuple-element.209, pred[8,2,128]{2,1,0:T(4,128)(4,1)S(1)} %broadcast_compare_fusion.2, ...), kind=kOutput, calls=%fused_computation.2.clone.1 | convolution fusion | flops 291840000 | bytes 11249664 | tf_op jit(solution)/shard_map/while/body/frbs,rbsc->frbc/dot_general | solution.py:82
  95.4 6.1 %fusion.78 = bf16[548,8,2,128]{3,2,0,1:T(2,128)(2,1)S(1)} fusion(bf16[548,8,6,128]{3,2,0,1:T(8,128)(2,1)} %get-tuple-element.208, s32[8,2]{1,0:T(8,128)S(1)} %copy.30), kind=kOutput, calls=%fused_computation.4.clone.1 | convolution fusion | flops 14590048 | bytes 8978496 | tf_op jit(solution)/shard_map/while/body/frqs,rbq->frbs/dot_general | solution.py:73
  101.6 5.9 %bitcast_add_fusion.4 = f32[548,8,2,128]{3,0,2,1:T(8,128)} fusion(f32[548,8,2,128]{3,0,2,1:T(8,128)} %get-tuple-element.192, bf16[548,8,2,128]{3,2,0,1:T(2,128)(2,1)S(1)} %fusion.78, s32[8,2,128]{2,1,0:T(2,128)S(1)} %get-tuple-element.209, pred[8,2,128]{2,1,0:T(4,128)(4,1)S(1)} %broadcast_compare_fusion.2, ...), kind=kOutput, calls=%fused_computation.2.clone.1 | convolution fusion | flops 291840000 | bytes 11249664 | tf_op jit(solution)/shard_map/while/body/frbs,rbsc->frbc/dot_general | solution.py:82
  108.2 6.1 %fusion.78 = bf16[548,8,2,128]{3,2,0,1:T(2,128)(2,1)S(1)} fusion(bf16[548,8,6,128]{3,2,0,1:T(8,128)(2,1)} %get-tuple-element.208, s32[8,2]{1,0:T(8,128)S(1)} %copy.30), kind=kOutput, calls=%fused_computation.4.clone.1 | convolution fusion | flops 14590048 | bytes 8978496 | tf_op jit(solution)/shard_map/while/body/frqs,rbq->frbs/dot_general | solution.py:73
  114.4 5.9 %bitcast_add_fusion.4 = f32[548,8,2,128]{3,0,2,1:T(8,128)} fusion(f32[548,8,2,128]{3,0,2,1:T(8,128)} %get-tuple-element.192, bf16[548,8,2,128]{3,2,0,1:T(2,128)(2,1)S(1)} %fusion.78, s32[8,2,128]{2,1,0:T(2,128)S(1)} %get-tuple-element.209, pred[8,2,128]{2,1,0:T(4,128)(4,1)S(1)} %broadcast_compare_fusion.2, ...), kind=kOutput, calls=%fused_computation.2.clone.1 | convolution fusion | flops 291840000 | bytes 11249664 | tf_op jit(solution)/shard_map/while/body/frbs,rbsc->frbc/dot_general | solution.py:82
  121.0 6.1 %fusion.78 = bf16[548,8,2,128]{3,2,0,1:T(2,128)(2,1)S(1)} fusion(bf16[548,8,6,128]{3,2,0,1:T(8,128)(2,1)} %get-tuple-element.208, s32[8,2]{1,0:T(8,128)S(1)} %copy.30), kind=kOutput, calls=%fused_computation.4.clone.1 | convolution fusion | flops 14590048 | bytes 8978496 | tf_op jit(solution)/shard_map/while/body/frqs,rbq->frbs/dot_general | solution.py:73
  127.2 5.9 %bitcast_add_fusion.4 = f32[548,8,2,128]{3,0,2,1:T(8,128)} fusion(f32[548,8,2,128]{3,0,2,1:T(8,128)} %get-tuple-element.192, bf16[548,8,2,128]{3,2,0,1:T(2,128)(2,1)S(1)} %fusion.78, s32[8,2,128]{2,1,0:T(2,128)S(1)} %get-tuple-element.209, pred[8,2,128]{2,1,0:T(4,128)(4,1)S(1)} %broadcast_compare_fusion.2, ...), kind=kOutput, calls=%fused_computation.2.clone.1 | convolution fusion | flops 291840000 | bytes 11249664 | tf_op jit(solution)/shard_map/while/body/frbs,rbsc->frbc/dot_general | solution.py:82
  133.7 3.7 %copy.26 = bf16[548,8,2,128]{3,1,2,0:T(8,128)(2,1)S(1)} copy(f32[548,8,2,128]{3,0,2,1:T(8,128)} %get-tuple-element.53) | data formatting | bytes 6733824 | tf_op jit(solution)/shard_map/while | solution.py:86
  140.9 5.1 %collective-permute-done.2 = bf16[548,2,256]{2,1,0:T(2,128)(2,1)S(1)} collective-permute-done((bf16[548,2,256]{2,1,0:T(2,128)(2,1)S(1)}, bf16[548,2,256]{2,1,0:T(2,128)(2,1)S(1)}, u32[]{:S(2)}, u32[]{:S(2)}) %collective-permute-start.2) | collective-permute-done | bytes 561184 | tf_op jit(solution)/shard_map/ppermute | solution.py:22
  146.0 3.9 %collective-permute-done.3 = bf16[548,2,256]{2,1,0:T(2,128)(2,1)S(1)} collective-permute-done((bf16[548,2,256]{2,1,0:T(2,128)(2,1)S(1)}, bf16[548,2,256]{2,1,0:T(2,128)(2,1)S(1)}, u32[]{:S(2)}, u32[]{:S(2)}) %collective-permute-start.3) | collective-permute-done | bytes 561184 | tf_op jit(solution)/shard_map/ppermute | solution.py:23
  149.9 4.8 %add_convert_fusion = bf16[548,8,256]{2,1,0:T(8,128)(2,1)S(1)} fusion(bf16[548,8,256]{2,1,0:T(8,128)(2,1)S(1)} %bitcast.83, bf16[548,2,256]{2,1,0:T(2,128)(2,1)S(1)} %collective-permute-done.3, bf16[548,2,256]{2,1,0:T(2,128)(2,1)S(1)} %collective-permute-done.2, f32[8,256]{1,0:T(8,128)S(1)} %get-tuple-element.116, f32[8,256]{1,0:T(8,128)S(1)} %get-tuple-element.117, ...), kind=kLoop, calls=%fused_computation.53 | loop fusion | flops 30302208 | bytes 5652480 | tf_op jit(solution)/shard_map/convert_element_type | solution.py:103
  154.7 20.1 %collective-permute-start.4 = (bf16[548,8,256]{2,1,0:T(8,128)(2,1)S(1)}, bf16[548,8,256]{2,1,0:T(8,128)(2,1)S(1)}, u32[]{:S(2)}, u32[]{:S(2)}) collective-permute-start(bf16[548,8,256]{2,1,0:T(8,128)(2,1)S(1)} %add_convert_fusion), channel_id=1, source_target_pairs={{0,8},{8,16},{16,24},{1,9},{9,17},{17,25},{2,10},{10,18},{18,26},{... | collective-permute-start | bytes 6733832 | tf_op jit(solution)/shard_map/ppermute | solution.py:31
  174.8 24.5 %collective-permute-done.4 = bf16[548,8,256]{2,1,0:T(8,128)(2,1)S(1)} collective-permute-done((bf16[548,8,256]{2,1,0:T(8,128)(2,1)S(1)}, bf16[548,8,256]{2,1,0:T(8,128)(2,1)S(1)}, u32[]{:S(2)}, u32[]{:S(2)}) %collective-permute-start.4) | collective-permute-done | bytes 2244640 | tf_op jit(solution)/shard_map/ppermute | solution.py:31
  199.4 2.1 %subtract_convert_fusion = bf16[548,8,256]{2,1,0:T(8,128)(2,1)} fusion(bf16[548,8,256]{2,1,0:T(8,128)(2,1)S(1)} %collective-permute-done.4, bf16[1,4,137,8,256]{4,3,2,1,0:T(8,128)(2,1)S(1)} %copy-done), kind=kLoop, calls=%fused_computation.52 | loop fusion | flops 4489216 | bytes 6733824 | tf_op jit(solution)/shard_map/convert_element_type | solution.py:105
  (41 shorter events, 9.6 us)
Async XLA Ops:
  0.0 53.6 %copy-start = (bf16[1,4,137,8,256]{4,3,2,1,0:T(8,128)(2,1)S(1)}, bf16[1,4,137,8,256]{4,3,2,1,0:T(8,128)(2,1)}, u32[]{:S(2)}) copy-start(bf16[1,4,137,8,256]{4,3,2,1,0:T(8,128)(2,1)} %param.10) | copy-start | bytes 6733828
  0.0 50.9 %collective-permute-start.1 = (bf16[548,8,256]{2,1,0:T(8,128)(2,1)}, bf16[548,8,256]{2,1,0:T(8,128)(2,1)}, u32[]{:S(2)}, u32[]{:S(2)}) collective-permute-start(bf16[548,8,256]{2,1,0:T(8,128)(2,1)} %bitcast.84), channel_id=1, source_target_pairs={{0,1},{1,0},{2,3},{3,2},{4,5},{5,4},{6,7},{7,6},{8,9},{9,8},{10,11... | collective-permute-start | bytes 6733832 | tf_op jit(solution)/shard_map/ppermute | solution.py:12
  2.0 50.2 %collective-permute-start = (bf16[548,8,256]{2,1,0:T(8,128)(2,1)}, bf16[548,8,256]{2,1,0:T(8,128)(2,1)}, u32[]{:S(2)}, u32[]{:S(2)}) collective-permute-start(bf16[548,8,256]{2,1,0:T(8,128)(2,1)} %bitcast.85), channel_id=1, source_target_pairs={{0,0},{1,1},{2,2},{3,3},{4,4},{5,5},{6,6},{7,7},{8,8},{9,9},{10,10... | collective-permute-start | bytes 6733832 | tf_op jit(solution)/shard_map/ppermute | solution.py:12
  133.7 7.1 %copy-start.1 = (s32[1,8,256]{2,1,0:T(8,128)S(1)}, s32[1,8,256]{2,1,0:T(8,128)}, u32[]{:S(2)}) copy-start(s32[1,8,256]{2,1,0:T(8,128)} %param.16) | copy-start | bytes 24580
  133.7 7.1 %copy-start.2 = (f32[1,8,256]{2,1,0:T(8,128)S(1)}, f32[1,8,256]{2,1,0:T(8,128)}, u32[]{:S(2)}) copy-start(f32[1,8,256]{2,1,0:T(8,128)} %param.17) | copy-start | bytes 24580
  138.2 7.8 %collective-permute-start.2 = (bf16[548,2,256]{2,1,0:T(2,128)(2,1)S(1)}, bf16[548,2,256]{2,1,0:T(2,128)(2,1)S(1)}, u32[]{:S(2)}, u32[]{:S(2)}) collective-permute-start(bf16[548,2,256]{2,1,0:T(2,128)(2,1)S(1)} %get-tuple-element.111), channel_id=1, source_target_pairs={{0,2},{2,4},{4,6},{1,3},{3,5},{5,7},{8,10},{10,12},{12,14},{9,11},... | collective-permute-start | bytes 1683464 | tf_op jit(solution)/shard_map/ppermute | solution.py:22
  139.5 10.3 %collective-permute-start.3 = (bf16[548,2,256]{2,1,0:T(2,128)(2,1)S(1)}, bf16[548,2,256]{2,1,0:T(2,128)(2,1)S(1)}, u32[]{:S(2)}, u32[]{:S(2)}) collective-permute-start(bf16[548,2,256]{2,1,0:T(2,128)(2,1)S(1)} %get-tuple-element.112), channel_id=1, source_target_pairs={{2,0},{4,2},{6,4},{3,1},{5,3},{7,5},{10,8},{12,10},{14,12},{11,9},... | collective-permute-start | bytes 1683464 | tf_op jit(solution)/shard_map/ppermute | solution.py:23
  154.7 44.7 %collective-permute-start.4 = (bf16[548,8,256]{2,1,0:T(8,128)(2,1)S(1)}, bf16[548,8,256]{2,1,0:T(8,128)(2,1)S(1)}, u32[]{:S(2)}, u32[]{:S(2)}) collective-permute-start(bf16[548,8,256]{2,1,0:T(8,128)(2,1)S(1)} %add_convert_fusion), channel_id=1, source_target_pairs={{0,8},{8,16},{16,24},{1,9},{9,17},{17,25},{2,10},{10,18},{18,26},{... | collective-permute-start | bytes 6733832 | tf_op jit(solution)/shard_map/ppermute | solution.py:31
where the time goes:
time: 204 us; the launch traced here: 201 us
  waiting for transfers between devices  60.9 us (30%)
  matrix products  59.9 us (29%)
  starting transfers between devices  42.6 us (21%)
  local copies, waits for them, and re-layouts  18.9 us (9%)
  other arithmetic  14.2 us (7%)
  loops' own time  4.14 us (2%)
    dot_general x5, matrix products, add_entry(): jnp.einsum('frqs,rbq->frbs', source, selector, preferred_element_type=jnp...  30.4 us
    dot_general x5, matrix products, add_entry(): jnp.einsum('frbs,rbsc->frbc', upstream, matrix, preferred_element_type=jn...  29.5 us
    ppermute x2, waiting for transfers between devices, shifted(): return lax.ppermute(value, axis, pairs)  27.4 us
    ppermute x1, waiting for transfers between devices, from_behind(): return lax.ppermute(block, axis, route)  24.5 us
    ppermute x1, starting transfers between devices, from_behind(): return lax.ppermute(block, axis, route)  20.1 us
    ppermute x2, starting transfers between devices, shifted(): return lax.ppermute(value, axis, pairs)  19.9 us
    unnamed x8, local copies, waits for them, and re-layouts  8.14 us
    ppermute x1, waiting for transfers between devices, with_halo(): before = lax.ppermute(last, axis, up)  5.12 us
  transfers between devices with their start and end apart: 5, of which 4 were waited for; matrix products, arithmetic and copies ran while one was open for 2% of the time, Pallas kernels for 0%

commit v1 on v0

v1 whole, which is shorter than its diff:
```python
import functools

import jax
import jax.numpy as jnp
from jax import lax
from jax.experimental import pallas as pl
from jax.experimental.pallas import tpu as pltpu
from jax.sharding import PartitionSpec as P

BLK = 128
CHUNK = 56
MESH = pl.DeviceIdType.MESH


def cubic_weights(fraction):
    return jnp.stack(
        [
            -fraction * (fraction - 1.0) * (fraction - 2.0) / 6.0,
            (fraction + 1.0) * (fraction - 1.0) * (fraction - 2.0) / 2.0,
            -(fraction + 1.0) * fraction * (fraction - 2.0) / 2.0,
            (fraction + 1.0) * fraction * (fraction - 1.0) / 6.0,
        ]
    )


def source_plan(blocks, devices):
    spread = blocks + blocks // 2
    count = min(3 * blocks, blocks * devices)
    slots, pieces, at = [None] * count, [], blocks
    for q in range(count):
        offset, block = divmod(q - spread, blocks)
        if offset % devices == 0:
            slots[q] = block
            continue
        if pieces and pieces[-1][0] == offset and pieces[-1][1] + pieces[-1][2] == block:
            pieces[-1][2] += 1
        else:
            pieces.append([offset, block, 1, at])
        slots[q] = at
        at += 1
    return slots, [tuple(piece) for piece in pieces], at


def kernel(plan, steps, depth, sizes, state, prm, prev, *scratch):
    _, pieces, n_src = plan
    n_tm, n_lat, n_lon = sizes
    n_pieces = len(pieces)
    own, remotes = scratch[0], scratch[1 : 1 + n_pieces]
    (
        flat, params, matrix, adv, f_end, ends, own_sem, x_send, x_recv,
        h_send, h_recv, t_send, t_recv, raw_send, p_send, p_recv,
    ) = scratch[1 + n_pieces :]
    rows, cols = state.shape[1:]
    tm, lat, lon = lax.axis_index("tm"), lax.axis_index("lat"), lax.axis_index("lon")

    helping = n_tm >= 3
    helper, helped = n_tm - 1, n_tm - 3
    half = steps // 2
    is_helper = tm == helper
    if helping:
        first = jnp.where(is_helper, half, 0)
        last = jnp.where(tm == helped, half, steps)
        target = jnp.where(is_helper, helped + 1, tm + 1)
    else:
        first = 0
        last = jnp.where(is_helper, 0, steps)
        target = tm + 1

    barrier = pltpu.get_barrier_semaphore()
    lon_near = sorted({p[0] % n_lon for p in pieces} | {-p[0] % n_lon for p in pieces})
    greeted = len(lon_near)
    for o in lon_near:
        pl.semaphore_signal(
            barrier, inc=1, device_id={"lon": lax.rem(lon + o, n_lon)}, device_id_type=MESH
        )

    def greet(condition, device):
        @pl.when(condition)
        def _():
            pl.semaphore_signal(barrier, inc=1, device_id=device, device_id_type=MESH)

        return jnp.where(condition, 1, 0)

    greeted += greet(lat > 0, {"lat": lat - 1}) + greet(lat < n_lat - 1, {"lat": lat + 1})
    greeted += greet(tm > 0, {"tm": tm - 1}) + greet(tm < n_tm - 1, {"tm": tm + 1})
    if helping:
        greeted += greet(tm == helped, {"tm": helper}) + greet(is_helper, {"tm": helped})
    pl.semaphore_wait(barrier, greeted)

    def begin(c):
        return jnp.minimum(c * CHUNK, depth - CHUNK)

    def own_copy(c):
        return pltpu.make_async_copy(state.at[pl.ds(begin(c), CHUNK)], own.at[c], own_sem.at[c])

    def raw_copy(c):
        return pltpu.make_async_remote_copy(
            src_ref=state.at[pl.ds(begin(c), CHUNK)], dst_ref=own.at[c], send_sem=raw_send.at[c],
            recv_sem=own_sem.at[c], device_id={"tm": helper}, device_id_type=MESH,
        )

    def prm_copy():
        return pltpu.make_async_remote_copy(
            src_ref=prm, dst_ref=params, send_sem=p_send, recv_sem=p_recv,
            device_id={"tm": helper}, device_id_type=MESH,
        )

    def x_copies(c):
        copies = []
        for i, (offset, block, number, _) in enumerate(pieces):
            copies.append(
                pltpu.make_async_remote_copy(
                    src_ref=own.at[c, :, :, pl.ds(block * BLK, number * BLK)],
                    dst_ref=remotes[i].at[c],
                    send_sem=x_send.at[i, c], recv_sem=x_recv.at[i, c],
                    device_id={"lon": lax.rem(lon - offset + 2 * n_lon, n_lon)},
                    device_id_type=MESH,
                )
            )
        return copies

    def halo_up(c):
        return pltpu.make_async_remote_copy(
            src_ref=adv.at[c, pl.ds(rows, 2)], dst_ref=adv.at[c, pl.ds(0, 2)],
            send_sem=h_send.at[0, c], recv_sem=h_recv.at[0, c],
            device_id={"lat": lat + 1}, device_id_type=MESH,
        )

    def halo_down(c):
        return pltpu.make_async_remote_copy(
            src_ref=adv.at[c, pl.ds(2, 2)], dst_ref=adv.at[c, pl.ds(rows + 2, 2)],
            send_sem=h_send.at[1, c], recv_sem=h_recv.at[1, c],
            device_id={"lat": lat - 1}, device_id_type=MESH,
        )

    rest = depth - (steps - 1) * CHUNK

    def end_copy(c, short):
        if short:
            source, place = ends.at[c, pl.ds(CHUNK - rest, rest)], pl.ds((steps - 1) * CHUNK, rest)
        else:
            source, place = ends.at[c], pl.ds(c * CHUNK, CHUNK)
        return pltpu.make_async_remote_copy(
            src_ref=source, dst_ref=prev.at[place], send_sem=t_send.at[c], recv_sem=t_recv.at[c],
            device_id={"tm": target}, device_id_type=MESH,
        )

    def each_end(c, act):
        @pl.when(c < steps - 1)
        def _():
            act(end_copy(c, False))

        @pl.when(c == steps - 1)
        def _():
            act(end_copy(c, True))

    def loop(low, high, act):
        lax.fori_loop(low, high, lambda c, _: (act(c), 0)[1], 0)

    local = jnp.logical_not(is_helper)

    @pl.when(local)
    def _():
        loop(first, last, lambda c: own_copy(c).start())
        pltpu.make_async_copy(prm, params, p_recv).start()

    if helping:

        @pl.when(tm == helped)
        def _():
            prm_copy().start()
            loop(half, steps, lambda c: raw_copy(c).start())

    def forward(c):
        own_copy(c).wait()
        for copy in x_copies(c):
            copy.start()

    ahead = jnp.where(is_helper, 2, steps)
    loop(first, jnp.minimum(first + ahead, last), forward)

    @pl.when(lat == 0)
    def _():
        adv[:, 0:2] = jnp.zeros((steps, 2, CHUNK, cols), adv.dtype)

    @pl.when(lat == n_lat - 1)
    def _():
        adv[:, rows + 2 : rows + 4] = jnp.zeros((steps, 2, CHUNK, cols), adv.dtype)

    def build(r):
        offset, slot = params[0, pl.ds(r, 1), :], params[1, pl.ds(r, 1), :]
        gap = lax.broadcasted_iota(jnp.int32, (BLK, cols), 0).astype(jnp.float32) - offset
        value = jnp.zeros((BLK, cols), jnp.float32)
        for node in range(4):
            weight = params[2 + node, pl.ds(r, 1), :]
            value = jnp.where(gap == node - 1.0, weight, value)
        for q in range(n_src):
            matrix[r, q * BLK : (q + 1) * BLK, :] = jnp.where(slot == q, value, 0.0).astype(
                jnp.bfloat16
            )

    def advect(c):
        for copy in x_copies(c):
            copy.wait_recv()
        at = 0
        for buffer in (own, *remotes):
            for b in range(buffer.shape[3] // BLK):
                part = buffer[c, :, :, b * BLK : (b + 1) * BLK].astype(jnp.float32)
                flat[at] = part.reshape(CHUNK * rows, BLK)
                at += 1
        for r in [0, 1, rows - 2, rows - 1] + list(range(2, rows - 2)):
            parts = [
                flat[q, pl.ds(r, CHUNK, stride=rows), :].astype(jnp.bfloat16)
                for q in range(n_src)
            ]
            total = jnp.dot(
                jnp.concatenate(parts, axis=1), matrix[r], preferred_element_type=jnp.float32
            )
            adv[c, r + 2] = total.astype(adv.dtype)

        @pl.when(lat < n_lat - 1)
        def _():
            halo_up(c).start()

        @pl.when(lat > 0)
        def _():
            halo_down(c).start()

    def finish(c):
        @pl.when(lat > 0)
        def _():
            halo_up(c).wait_recv()

        @pl.when(lat < n_lat - 1)
        def _():
            halo_down(c).wait_recv()

        for r in range(rows):
            total = None
            for shift in range(5):
                term = params[6 + shift, r : r + 1, :] * adv[c, r + shift].astype(jnp.float32)
                total = term if total is None else total + term
            for b in range(cols // BLK):
                f_end[b, pl.ds(r, CHUNK, stride=rows), :] = total[:, b * BLK : (b + 1) * BLK]
        for b in range(cols // BLK):
            part = f_end[b].reshape(CHUNK, rows, BLK).astype(ends.dtype)
            ends[c, :, :, b * BLK : (b + 1) * BLK] = part
        each_end(c, lambda copy: copy.start())

    def step(c):
        @pl.when(c + ahead < last)
        def _():
            forward(c + ahead)

        @pl.when(c < last)
        def _():
            advect(c)

        @pl.when(c > first)
        def _():
            finish(c - 1)

    def settle(c):
        for copy in x_copies(c):
            copy.wait_send()

        @pl.when(lat < n_lat - 1)
        def _():
            halo_up(c).wait_send()

        @pl.when(lat > 0)
        def _():
            halo_down(c).wait_send()

        each_end(c, lambda copy: copy.wait_send())

    @pl.when(first < last)
    def _():
        pltpu.make_async_copy(prm, params, p_recv).wait()
        loop(0, rows, build)
        loop(first, last + 1, step)
        loop(first, last, settle)

    if helping:

        @pl.when(tm == helped)
        def _():
            prm_copy().wait_send()
            loop(half, steps, lambda c: raw_copy(c).wait_send())

    @pl.when(tm > 0)
    def _():
        loop(0, steps, lambda c: each_end(c, lambda copy: copy.wait_recv()))


def body(sizes, state, band_counts, dep_blocks, lon_entry, lon_offset, lon_frac, lat_offset, lat_frac):
    fields_n, levels, rows, cols = state.shape[1:]
    depth, blocks = fields_n * levels, cols // BLK
    n_tm, n_lat, n_lon = sizes
    plan = source_plan(blocks, n_lon)
    slots, pieces, n_src = plan
    steps = -(-depth // CHUNK)
    flat = state.reshape(depth, rows, cols)

    spread = blocks + blocks // 2
    placed = (dep_blocks[0] - lax.axis_index("lon") * blocks + spread) % (blocks * n_lon)
    slot_of = jnp.zeros_like(placed)
    for q, slot in enumerate(slots):
        slot_of = jnp.where(placed == q, slot, slot_of)
    entry = lon_entry[0] % band_counts[0, 0]
    chosen = jnp.zeros((rows, blocks, BLK), jnp.int32)
    for k in range(dep_blocks.shape[-1]):
        chosen = jnp.where(entry.reshape(rows, blocks, BLK) == k, slot_of[:, :, k : k + 1], chosen)
    chosen = chosen.reshape(rows, cols)
    weights = cubic_weights(lon_frac[0]).astype(jnp.bfloat16).astype(jnp.float32)
    lat_weights = cubic_weights(lat_frac[0])
    coefficients = []
    for shift in range(-2, 3):
        coefficient = jnp.zeros((rows, cols), jnp.float32)
        for node in range(4):
            coefficient = coefficient + jnp.where(
                lat_offset[0] + node - 1 == shift, lat_weights[node], 0.0
            )
        coefficients.append(coefficient)
    prm = jnp.stack(
        [lon_offset[0].astype(jnp.float32), chosen.astype(jnp.float32)]
        + [weights[m] for m in range(4)]
        + coefficients
    )

    dma = pltpu.SemaphoreType.DMA
    n_pieces = len(pieces)
    prev = pl.pallas_call(
        functools.partial(kernel, plan, steps, depth, sizes),
        out_shape=jax.ShapeDtypeStruct(flat.shape, flat.dtype),
        in_specs=[pl.BlockSpec(memory_space=pl.ANY)] * 2,
        out_specs=pl.BlockSpec(memory_space=pl.ANY),
        scratch_shapes=[
            pltpu.VMEM((steps, CHUNK, rows, cols), flat.dtype),
            *[pltpu.VMEM((steps, CHUNK, rows, p[2] * BLK), flat.dtype) for p in pieces],
            pltpu.VMEM((n_src, CHUNK * rows, BLK), jnp.float32),
            pltpu.VMEM(prm.shape, jnp.float32),
            pltpu.VMEM((rows, n_src * BLK, cols), jnp.bfloat16),
            pltpu.VMEM((steps, rows + 4, CHUNK, cols), flat.dtype),
            pltpu.VMEM((blocks, CHUNK * rows, BLK), jnp.float32),
            pltpu.VMEM((steps, CHUNK, rows, cols), flat.dtype),
            dma((steps,)),
            dma((n_pieces, steps)),
            dma((n_pieces, steps)),
            dma((2, steps)),
            dma((2, steps)),
            dma((steps,)),
            dma((steps,)),
            dma((steps,)),
            dma(()),
            dma(()),
        ],
        compiler_params=pltpu.CompilerParams(
            collective_id=0, has_side_effects=True, vmem_limit_bytes=40 * 1024 * 1024
        ),
    )(flat, prm)
    moved = jnp.where(lax.axis_index("tm") > 0, prev.astype(jnp.float32), 0.0)
    misfit = (flat.astype(jnp.float32) - moved).astype(state.dtype)
    return misfit.reshape(state.shape)


def solution(mesh):
    placed = (
        P("tm", None, None, "lat", "lon"),
        P("tm", "lat"),
        P("tm", "lat", "lon", None),
        P("tm", "lat", "lon"),
        P("tm", "lat", "lon"),
        P("tm", "lat", "lon"),
        P("tm", "lat", "lon"),
        P("tm", "lat", "lon"),
    )
    sizes = tuple(mesh.shape[name] for name in ("tm", "lat", "lon"))
    return jax.shard_map(
        functools.partial(body, sizes),
        mesh=mesh,
        in_specs=placed,
        out_specs=P("tm", None, None, "lat", "lon"),
        check_vma=False,
    )
```

time: 204 us -> 63.1 us (0.31)
  the two profiles are of different devices: /device:TPU:1 before, /device:TPU:5 now
where the time goes in v1:
time: 63.1 us; the launch traced here: 62.1 us
  Pallas kernels  51.6 us (82%)
  other arithmetic  8.17 us (13%)
  local copies, waits for them, and re-layouts  1.63 us (3%)
  between operations  0.71 us (1%)
    pallas_call x1, Pallas kernels, body(): pl.pallas_call(functools.partial(kernel, plan, steps, depth, sizes), out_...  51.6 us
    unnamed x6, other arithmetic  3.64 us
    convert_element_type x1, other arithmetic, body(): misfit = (flat.astype(jnp.float32) - moved).astype(state.dtype)  2.23 us
    unnamed x2, local copies, waits for them, and re-layouts  1.63 us

profile of v1, /device:TPU:5, one launch (start us, length us, event | category | flops | bytes accessed | tf_op | source)
XLA Modules:
  0.0 62.1 jit_solution(7645789175701739835)
XLA Ops:
  0.7 0.7 %compare_select_fusion.5 = s32[8,2,6]{0,1,2:T(2,128)S(1)} fusion(s32[1,8,2,6]{1,2,3,0:T(2,128)} %param.10, s32[]{:T(128)S(6)} %mul.99), kind=kLoop, calls=%fused_computation.15 | loop fusion | flops 2016 | bytes 772 | tf_op jit(solution)/shard_map/jit(_where)/select_n | solution.py:309
  1.4 0.7 %constant_dynamic-update-slice_fusion.6 = f32[11,8,256]{2,1,0:T(8,128)S(1)} fusion(s32[1,8,256]{2,1,0:T(8,128)} %param.12), kind=kLoop, calls=%fused_computation.8 | loop fusion | flops 2047 | bytes 16384
  2.1 0.8 %multiply_convert_fusion = (bf16[1,8,256]{2,1,0:T(8,128)(2,1)S(1)}, bf16[1,8,256]{2,1,0:T(8,128)(2,1)S(1)}, bf16[1,8,256]{2,1,0:T(8,128)(2,1)S(1)}, bf16[1,8,256]{2,1,0:T(8,128)(2,1)S(1)}, f32[11,8,256]{2,1,0:T(8,128)S(1)}) fusion(f32[1,8,256]{2,1,0:T(8,128)} %param.13, f32[11,8,256]{2,1,0:T(8,128)S(1)} %constant_dynamic-update-slice_fusion.6, ...), kind=kLoop, calls=%fused_computation.48 | loop fusion | flops 83968 | bytes 47109 | tf_op jit(solution)/shard_map/convert
  3.0 0.7 %constant_dynamic-update-slice_fusion.4 = f32[11,8,256]{2,1,0:T(8,128)S(1)} fusion(f32[11,8,256]{2,1,0:T(8,128)S(1)} %convert_dynamic-update-slice_fusion, s32[1,8,256]{2,1,0:T(8,128)} %param.14, f32[1,8,256]{2,1,0:T(8,128)} %param.15), kind=kLoop, calls=%fused_computation.6 | loop fusion | flops 63488 | bytes 24576
  3.7 0.7 %constant_dynamic-update-slice_fusion.3 = f32[11,8,256]{2,1,0:T(8,128)S(1)} fusion(f32[11,8,256]{2,1,0:T(8,128)S(1)} %constant_dynamic-update-slice_fusion.4, s32[1,8,256]{2,1,0:T(8,128)} %param.14, f32[1,8,256]{2,1,0:T(8,128)} %param.15), kind=kLoop, calls=%fused_computation.5 | loop fusion | flops 63488 | bytes 24576
  4.4 0.7 %constant_dynamic-update-slice_fusion.2 = f32[11,8,256]{2,1,0:T(8,128)S(1)} fusion(f32[11,8,256]{2,1,0:T(8,128)S(1)} %constant_dynamic-update-slice_fusion.3, s32[1,8,256]{2,1,0:T(8,128)} %param.14, f32[1,8,256]{2,1,0:T(8,128)} %param.15), kind=kLoop, calls=%fused_computation.4 | loop fusion | flops 63488 | bytes 24576
  5.2 0.7 %constant_dynamic-update-slice_fusion.1 = f32[11,8,256]{2,1,0:T(8,128)S(1)} fusion(f32[11,8,256]{2,1,0:T(8,128)S(1)} %constant_dynamic-update-slice_fusion.2, s32[1,8,256]{2,1,0:T(8,128)} %param.14, f32[1,8,256]{2,1,0:T(8,128)} %param.15), kind=kLoop, calls=%fused_computation.3 | loop fusion | flops 63488 | bytes 24576
  5.9 0.7 %constant_dynamic-update-slice_fusion.prm = f32[11,8,256]{2,1,0:T(8,128)S(1)} fusion(f32[11,8,256]{2,1,0:T(8,128)S(1)} %constant_dynamic-update-slice_fusion.1, s32[1,8,256]{2,1,0:T(8,128)} %param.14, f32[1,8,256]{2,1,0:T(8,128)} %param.15), kind=kLoop, calls=%fused_computation.2 | loop fusion | flops 63488 | bytes 24576 | tf_op jit(solution)/shard_map/stack | solution.py:325
  6.6 0.0 copy-start
  6.6 1.6 %copy-done = bf16[1,4,137,8,256]{4,3,2,1,0:T(8,128)(2,1)S(1)} copy-done((bf16[1,4,137,8,256]{4,3,2,1,0:T(8,128)(2,1)S(1)}, bf16[1,4,137,8,256]{4,3,2,1,0:T(8,128)(2,1)}, u32[]{:S(2)}) %copy-start) | copy-done | bytes 2244632
  8.3 51.6 %shard_map.82 = bf16[548,8,256]{2,1,0:T(8,128)(2,1)S(1)} custom-call(bf16[548,8,256]{2,1,0:T(8,128)(2,1)S(1)} %bitcast.46, f32[11,8,256]{2,1,0:T(8,128)S(1)} %constant_dynamic-update-slice_fusion.prm), custom_call_target="tpu_custom_call" | custom-call | tf_op jit(solution)/shard_map/pallas_call | solution.py:333
  59.9 2.2 %subtract_convert_fusion = bf16[548,8,256]{2,1,0:T(8,128)(2,1)} fusion(bf16[548,8,256]{2,1,0:T(8,128)(2,1)S(1)} %shard_map.82, pred[]{:T(512)S(6)} %gt.3, bf16[1,4,137,8,256]{4,3,2,1,0:T(8,128)(2,1)S(1)} %copy-done), kind=kLoop, calls=%fused_computation | loop fusion | flops 5611520 | bytes 6733825 | tf_op jit(solution)/shard_map/convert_element_type | solution.py:363
  (2 shorter events, 0.0 us)
Async XLA Ops:
  6.6 1.6 %copy-start = (bf16[1,4,137,8,256]{4,3,2,1,0:T(8,128)(2,1)S(1)}, bf16[1,4,137,8,256]{4,3,2,1,0:T(8,128)(2,1)}, u32[]{:S(2)}) copy-start(bf16[1,4,137,8,256]{4,3,2,1,0:T(8,128)(2,1)} %param.8) | copy-start | bytes 6733828

commit v2 on v1

--- a/solution.py
+++ b/solution.py
@@ -8,19 +8,17 @@
 from jax.sharding import PartitionSpec as P
 
 BLK = 128
-CHUNK = 56
+CHUNK = 72
 MESH = pl.DeviceIdType.MESH
 
 
 def cubic_weights(fraction):
-    return jnp.stack(
-        [
-            -fraction * (fraction - 1.0) * (fraction - 2.0) / 6.0,
-            (fraction + 1.0) * (fraction - 1.0) * (fraction - 2.0) / 2.0,
-            -(fraction + 1.0) * fraction * (fraction - 2.0) / 2.0,
-            (fraction + 1.0) * fraction * (fraction - 1.0) / 6.0,
-        ]
-    )
+    return [
+        -fraction * (fraction - 1.0) * (fraction - 2.0) / 6.0,
+        (fraction + 1.0) * (fraction - 1.0) * (fraction - 2.0) / 2.0,
+        -(fraction + 1.0) * fraction * (fraction - 2.0) / 2.0,
+        (fraction + 1.0) * fraction * (fraction - 1.0) / 6.0,
+    ]
 
 
 def source_plan(blocks, devices):
@@ -41,14 +39,15 @@
     return slots, [tuple(piece) for piece in pieces], at
 
 
-def kernel(plan, steps, depth, sizes, state, prm, prev, *scratch):
-    _, pieces, n_src = plan
+def kernel(plan, steps, depth, sizes, state, counts, lists, *rest_refs):
+    slots, pieces, n_src = plan
+    arrays, prev, scratch = rest_refs[:5], rest_refs[5], rest_refs[6:]
     n_tm, n_lat, n_lon = sizes
     n_pieces = len(pieces)
     own, remotes = scratch[0], scratch[1 : 1 + n_pieces]
     (
-        flat, params, matrix, adv, f_end, ends, own_sem, x_send, x_recv,
-        h_send, h_recv, t_send, t_recv, raw_send, p_send, p_recv,
+        counts_s, lists_s, *arrays_v, flat, params, matrix, adv, f_end, ends, own_sem, x_send, x_recv,
+        h_send, h_recv, t_send, t_recv, raw_send, p_send, p_recv, a_sem,
     ) = scratch[1 + n_pieces :]
     rows, cols = state.shape[1:]
     tm, lat, lon = lax.axis_index("tm"), lax.axis_index("lat"), lax.axis_index("lon")
@@ -56,6 +55,7 @@
     helping = n_tm >= 3
     helper, helped = n_tm - 1, n_tm - 3
     half = steps // 2
+    rest = depth - (steps - 1) * CHUNK
     is_helper = tm == helper
     if helping:
         first = jnp.where(is_helper, half, 0)
@@ -101,17 +101,18 @@
 
     def prm_copy():
         return pltpu.make_async_remote_copy(
-            src_ref=prm, dst_ref=params, send_sem=p_send, recv_sem=p_recv,
+            src_ref=params, dst_ref=params, send_sem=p_send, recv_sem=p_recv,
             device_id={"tm": helper}, device_id_type=MESH,
         )
 
-    def x_copies(c):
+    def x_copies(c, short):
+        part = pl.ds(CHUNK - rest, rest) if short else pl.ds(0, CHUNK)
         copies = []
         for i, (offset, block, number, _) in enumerate(pieces):
             copies.append(
                 pltpu.make_async_remote_copy(
-                    src_ref=own.at[c, :, :, pl.ds(block * BLK, number * BLK)],
-                    dst_ref=remotes[i].at[c],
+                    src_ref=own.at[c, part, :, pl.ds(block * BLK, number * BLK)],
+                    dst_ref=remotes[i].at[c, part],
                     send_sem=x_send.at[i, c], recv_sem=x_recv.at[i, c],
                     device_id={"lon": lax.rem(lon - offset + 2 * n_lon, n_lon)},
                     device_id_type=MESH,
@@ -119,6 +120,17 @@
             )
         return copies
 
+    def each_x(c, act):
+        @pl.when(c < steps - 1)
+        def _():
+            for copy in x_copies(c, False):
+                act(copy)
+
+        @pl.when(c == steps - 1)
+        def _():
+            for copy in x_copies(c, True):
+                act(copy)
+
     def halo_up(c):
         return pltpu.make_async_remote_copy(
             src_ref=adv.at[c, pl.ds(rows, 2)], dst_ref=adv.at[c, pl.ds(0, 2)],
@@ -132,8 +144,6 @@
             send_sem=h_send.at[1, c], recv_sem=h_recv.at[1, c],
             device_id={"lat": lat - 1}, device_id_type=MESH,
         )
-
-    rest = depth - (steps - 1) * CHUNK
 
     def end_copy(c, short):
         if short:
@@ -157,24 +167,30 @@
     def loop(low, high, act):
         lax.fori_loop(low, high, lambda c, _: (act(c), 0)[1], 0)
 
+    aux = [
+        pltpu.make_async_copy(source, place, a_sem.at[i])
+        for i, (source, place) in enumerate(
+            [(counts, counts_s), (lists, lists_s)]
+            + [(array.at[0], place) for array, place in zip(arrays, arrays_v)]
+        )
+    ]
     local = jnp.logical_not(is_helper)
 
     @pl.when(local)
     def _():
         loop(first, last, lambda c: own_copy(c).start())
-        pltpu.make_async_copy(prm, params, p_recv).start()
+        for copy in aux:
+            copy.start()
 
     if helping:
 
         @pl.when(tm == helped)
         def _():
-            prm_copy().start()
             loop(half, steps, lambda c: raw_copy(c).start())
 
     def forward(c):
         own_copy(c).wait()
-        for copy in x_copies(c):
-            copy.start()
+        each_x(c, lambda copy: copy.start())
 
     ahead = jnp.where(is_helper, 2, steps)
     loop(first, jnp.minimum(first + ahead, last), forward)
@@ -186,6 +202,39 @@
     @pl.when(lat == n_lat - 1)
     def _():
         adv[:, rows + 2 : rows + 4] = jnp.zeros((steps, 2, CHUNK, cols), adv.dtype)
+
+    def prepare():
+        for copy in aux:
+            copy.wait()
+        entry, offset, lon_fraction, lat_shift, lat_fraction = [v[...] for v in arrays_v]
+        per_list = lists.shape[-1]
+        for _ in range((per_list - 1) // 2):
+            entry = jnp.where(entry >= counts_s[0, 0], entry - counts_s[0, 0], entry)
+        blocks = cols // BLK
+        total = blocks * n_lon
+        for r in range(rows):
+            for g in range(blocks):
+                wanted = entry[r : r + 1, g * BLK : (g + 1) * BLK]
+                chosen = jnp.zeros((1, BLK), jnp.int32)
+                for k in range(per_list):
+                    q = lists_s[0, r, g, k] - lon * blocks + blocks + blocks // 2 + total
+                    q = lax.rem(q, total)
+                    slot = jnp.int32(slots[0])
+                    for i in range(1, len(slots)):
+                        slot = jnp.where(q == i, slots[i], slot)
+                    chosen = jnp.where(wanted == k, slot, chosen)
+                params[1, r : r + 1, g * BLK : (g + 1) * BLK] = chosen.astype(jnp.float32)
+        params[0] = offset.astype(jnp.float32)
+        for node, weight in enumerate(cubic_weights(lon_fraction)):
+            params[2 + node] = weight.astype(jnp.bfloat16).astype(jnp.float32)
+        lat_weights = cubic_weights(lat_fraction)
+        for shift in range(-2, 3):
+            coefficient = jnp.zeros((rows, cols), jnp.float32)
+            for node in range(4):
+                coefficient = coefficient + jnp.where(
+                    lat_shift + node - 1 == shift, lat_weights[node], 0.0
+                )
+            params[8 + shift] = coefficient
 
     def build(r):
         offset, slot = params[0, pl.ds(r, 1), :], params[1, pl.ds(r, 1), :]
@@ -200,8 +249,7 @@
             )
 
     def advect(c):
-        for copy in x_copies(c):
-            copy.wait_recv()
+        each_x(c, lambda copy: copy.wait_recv())
         at = 0
         for buffer in (own, *remotes):
             for b in range(buffer.shape[3] // BLK):
@@ -261,8 +309,7 @@
             finish(c - 1)
 
     def settle(c):
-        for copy in x_copies(c):
-            copy.wait_send()
+        each_x(c, lambda copy: copy.wait_send())
 
         @pl.when(lat < n_lat - 1)
         def _():
@@ -276,7 +323,17 @@
 
     @pl.when(first < last)
     def _():
-        pltpu.make_async_copy(prm, params, p_recv).wait()
+        pl.when(local)(prepare)
+        if helping:
+
+            @pl.when(tm == helped)
+            def _():
+                prm_copy().start()
+
+            @pl.when(is_helper)
+            def _():
+                prm_copy().wait_recv()
+
         loop(0, rows, build)
         loop(first, last + 1, step)
         loop(first, last, settle)
@@ -298,48 +355,28 @@
     depth, blocks = fields_n * levels, cols // BLK
     n_tm, n_lat, n_lon = sizes
     plan = source_plan(blocks, n_lon)
-    slots, pieces, n_src = plan
+    _, pieces, n_src = plan
     steps = -(-depth // CHUNK)
     flat = state.reshape(depth, rows, cols)
-
-    spread = blocks + blocks // 2
-    placed = (dep_blocks[0] - lax.axis_index("lon") * blocks + spread) % (blocks * n_lon)
-    slot_of = jnp.zeros_like(placed)
-    for q, slot in enumerate(slots):
-        slot_of = jnp.where(placed == q, slot, slot_of)
-    entry = lon_entry[0] % band_counts[0, 0]
-    chosen = jnp.zeros((rows, blocks, BLK), jnp.int32)
-    for k in range(dep_blocks.shape[-1]):
-        chosen = jnp.where(entry.reshape(rows, blocks, BLK) == k, slot_of[:, :, k : k + 1], chosen)
-    chosen = chosen.reshape(rows, cols)
-    weights = cubic_weights(lon_frac[0]).astype(jnp.bfloat16).astype(jnp.float32)
-    lat_weights = cubic_weights(lat_frac[0])
-    coefficients = []
-    for shift in range(-2, 3):
-        coefficient = jnp.zeros((rows, cols), jnp.float32)
-        for node in range(4):
-            coefficient = coefficient + jnp.where(
-                lat_offset[0] + node - 1 == shift, lat_weights[node], 0.0
-            )
-        coefficients.append(coefficient)
-    prm = jnp.stack(
-        [lon_offset[0].astype(jnp.float32), chosen.astype(jnp.float32)]
-        + [weights[m] for m in range(4)]
-        + coefficients
-    )
 
     dma = pltpu.SemaphoreType.DMA
     n_pieces = len(pieces)
     prev = pl.pallas_call(
         functools.partial(kernel, plan, steps, depth, sizes),
         out_shape=jax.ShapeDtypeStruct(flat.shape, flat.dtype),
-        in_specs=[pl.BlockSpec(memory_space=pl.ANY)] * 2,
+        in_specs=[pl.BlockSpec(memory_space=pltpu.HBM)] * 8,
         out_specs=pl.BlockSpec(memory_space=pl.ANY),
         scratch_shapes=[
             pltpu.VMEM((steps, CHUNK, rows, cols), flat.dtype),
             *[pltpu.VMEM((steps, CHUNK, rows, p[2] * BLK), flat.dtype) for p in pieces],
+            pltpu.SMEM(band_counts.shape, jnp.int32),
+            pltpu.SMEM(dep_blocks.shape, jnp.int32),
+            *[
+                pltpu.VMEM((rows, cols), kind.dtype)
+                for kind in (lon_entry, lon_offset, lon_frac, lat_offset, lat_frac)
+            ],
             pltpu.VMEM((n_src, CHUNK * rows, BLK), jnp.float32),
-            pltpu.VMEM(prm.shape, jnp.float32),
+            pltpu.VMEM((11, rows, cols), jnp.float32),
             pltpu.VMEM((rows, n_src * BLK, cols), jnp.bfloat16),
             pltpu.VMEM((steps, rows + 4, CHUNK, cols), flat.dtype),
             pltpu.VMEM((blocks, CHUNK * rows, BLK), jnp.float32),
@@ -354,11 +391,12 @@
             dma((steps,)),
             dma(()),
             dma(()),
+            dma((7,)),
         ],
         compiler_params=pltpu.CompilerParams(
             collective_id=0, has_side_effects=True, vmem_limit_bytes=40 * 1024 * 1024
         ),
-    )(flat, prm)
+    )(flat, band_counts, dep_blocks, lon_entry, lon_offset, lon_frac, lat_offset, lat_frac)
     moved = jnp.where(lax.axis_index("tm") > 0, prev.astype(jnp.float32), 0.0)
     misfit = (flat.astype(jnp.float32) - moved).astype(state.dtype)
     return misfit.reshape(state.shape)

time: 63.1 us -> 61.3 us (0.971)
  the two profiles are of different devices: /device:TPU:5 before, /device:TPU:1 now
where the time goes in v2:
time: 61.3 us; the launch traced here: 60.6 us
  Pallas kernels  49 us (80%)
  local copies, waits for them, and re-layouts  7.25 us (12%)
  other arithmetic  3.65 us (6%)
  between operations  0.68 us (1%)
    pallas_call x1, Pallas kernels, body(): pl.pallas_call(functools.partial(kernel, plan, steps, depth, sizes), out_...  49 us
    unnamed x17, local copies, waits for them, and re-layouts  7.25 us
    convert_element_type x1, other arithmetic, body(): misfit = (flat.astype(jnp.float32) - moved).astype(state.dtype)  3.65 us

profile of v2, /device:TPU:1, one launch (start us, length us, event | category | flops | bytes accessed | tf_op | source)
XLA Modules:
  0.0 60.6 jit_solution(15798412198150048212)
XLA Ops:
  0.0 0.8 %copy.9.lists = s32[1,8,2,6]{3,2,1,0:T(2,128)S(1)} copy(s32[1,8,2,6]{1,2,3,0:T(2,128)} %param.10) | data formatting | bytes 768 | tf_op args[2]
  1.4 0.0 copy-start
  1.4 1.6 %copy-done = bf16[1,4,137,8,256]{4,3,2,1,0:T(8,128)(2,1)S(1)} copy-done((bf16[1,4,137,8,256]{4,3,2,1,0:T(8,128)(2,1)S(1)}, bf16[1,4,137,8,256]{4,3,2,1,0:T(8,128)(2,1)}, u32[]{:S(2)}) %copy-start) | copy-done | bytes 2244632
  3.1 0.0 copy-start.3
  3.1 0.7 %copy-done.3 = s32[1,8,256]{2,1,0:T(8,128)S(1)} copy-done((s32[1,8,256]{2,1,0:T(8,128)S(1)}, s32[1,8,256]{2,1,0:T(8,128)}, u32[]{:S(2)}) %copy-start.3) | copy-done | bytes 8216
  3.8 0.0 copy-start.4
  3.8 0.7 %copy-done.4 = s32[1,8,256]{2,1,0:T(8,128)S(1)} copy-done((s32[1,8,256]{2,1,0:T(8,128)S(1)}, s32[1,8,256]{2,1,0:T(8,128)}, u32[]{:S(2)}) %copy-start.4) | copy-done | bytes 8216
  4.5 0.0 copy-start.5
  4.5 0.7 %copy-done.5 = f32[1,8,256]{2,1,0:T(8,128)S(1)} copy-done((f32[1,8,256]{2,1,0:T(8,128)S(1)}, f32[1,8,256]{2,1,0:T(8,128)}, u32[]{:S(2)}) %copy-start.5) | copy-done | bytes 8216
  5.2 0.0 copy-start.6
  5.2 0.7 %copy-done.6 = s32[1,8,256]{2,1,0:T(8,128)S(1)} copy-done((s32[1,8,256]{2,1,0:T(8,128)S(1)}, s32[1,8,256]{2,1,0:T(8,128)}, u32[]{:S(2)}) %copy-start.6) | copy-done | bytes 8216
  5.9 0.0 copy-start.7
  5.9 0.7 %copy-done.7 = f32[1,8,256]{2,1,0:T(8,128)S(1)} copy-done((f32[1,8,256]{2,1,0:T(8,128)S(1)}, f32[1,8,256]{2,1,0:T(8,128)}, u32[]{:S(2)}) %copy-start.7) | copy-done | bytes 8216
  6.6 0.0 copy-start.1
  6.6 49.0 %shard_map.82 = bf16[548,8,256]{2,1,0:T(8,128)(2,1)S(1)} custom-call(bf16[548,8,256]{2,1,0:T(8,128)(2,1)S(1)} %bitcast.3, s32[1,1]{1,0:T(1,128)S(6)} %copy.10.counts, s32[1,8,2,6]{3,2,1,0:T(2,128)S(1)} %copy.9.lists, s32[1,8,256]{2,1,0:T(8,128)S(1)} %copy-done.3, s32[1,8,256]{2,1,0:T(8,128)S(1)} %copy-done.4, f32[1,8,256]{2,1,0:T(8,128)S(1)} %copy-done.5, ...), custom_call_target="tpu_custom_call" | custom-call | tf_op jit(solution)/shard_map/pallas_call | solution.py:364
  55.6 0.0 copy-start.2
  55.6 1.4 %copy-done.2 = bf16[548,8,256]{2,1,0:T(8,128)(2,1)} copy-done((bf16[548,8,256]{2,1,0:T(8,128)(2,1)}, bf16[548,8,256]{2,1,0:T(8,128)(2,1)S(1)}, u32[]{:S(2)}) %copy-start.2) | copy-done | bytes 2244632
  57.0 0.0 copy-done.1
  57.0 3.7 %subtract_convert_fusion = bf16[548,8,256]{2,1,0:T(8,128)(2,1)} fusion(bf16[548,8,256]{2,1,0:T(8,128)(2,1)} %copy-done.2, pred[]{:T(512)S(6)} %gt.3, bf16[1,4,137,8,256]{4,3,2,1,0:T(8,128)(2,1)S(1)} %copy-done.1), kind=kLoop, calls=%fused_computation | loop fusion | flops 5611520 | bytes 6733825 | tf_op jit(solution)/shard_map/convert_element_type | solution.py:401
Async XLA Ops:
  1.4 1.6 %copy-start = (bf16[1,4,137,8,256]{4,3,2,1,0:T(8,128)(2,1)S(1)}, bf16[1,4,137,8,256]{4,3,2,1,0:T(8,128)(2,1)}, u32[]{:S(2)}) copy-start(bf16[1,4,137,8,256]{4,3,2,1,0:T(8,128)(2,1)} %param.8) | copy-start | bytes 6733828
  3.1 0.7 %copy-start.3 = (s32[1,8,256]{2,1,0:T(8,128)S(1)}, s32[1,8,256]{2,1,0:T(8,128)}, u32[]{:S(2)}) copy-start(s32[1,8,256]{2,1,0:T(8,128)} %rest_refs_0_.1) | copy-start | bytes 24580
  3.8 0.7 %copy-start.4 = (s32[1,8,256]{2,1,0:T(8,128)S(1)}, s32[1,8,256]{2,1,0:T(8,128)}, u32[]{:S(2)}) copy-start(s32[1,8,256]{2,1,0:T(8,128)} %rest_refs_1_.1) | copy-start | bytes 24580
  4.5 0.7 %copy-start.5 = (f32[1,8,256]{2,1,0:T(8,128)S(1)}, f32[1,8,256]{2,1,0:T(8,128)}, u32[]{:S(2)}) copy-start(f32[1,8,256]{2,1,0:T(8,128)} %rest_refs_2_.1) | copy-start | bytes 24580
  5.2 0.7 %copy-start.6 = (s32[1,8,256]{2,1,0:T(8,128)S(1)}, s32[1,8,256]{2,1,0:T(8,128)}, u32[]{:S(2)}) copy-start(s32[1,8,256]{2,1,0:T(8,128)} %rest_refs_3_.1) | copy-start | bytes 24580
  5.9 0.7 %copy-start.7 = (f32[1,8,256]{2,1,0:T(8,128)S(1)}, f32[1,8,256]{2,1,0:T(8,128)}, u32[]{:S(2)}) copy-start(f32[1,8,256]{2,1,0:T(8,128)} %rest_refs_4_.1) | copy-start | bytes 24580
  6.6 50.4 %copy-start.1 = (bf16[1,4,137,8,256]{4,3,2,1,0:T(8,128)(2,1)S(1)}, bf16[1,4,137,8,256]{4,3,2,1,0:T(8,128)(2,1)}, u32[]{:S(2)}) copy-start(bf16[1,4,137,8,256]{4,3,2,1,0:T(8,128)(2,1)} %param.8) | copy-start | bytes 6733828
  55.6 1.4 %copy-start.2 = (bf16[548,8,256]{2,1,0:T(8,128)(2,1)}, bf16[548,8,256]{2,1,0:T(8,128)(2,1)S(1)}, u32[]{:S(2)}) copy-start(bf16[548,8,256]{2,1,0:T(8,128)(2,1)S(1)} %shard_map.82) | copy-start | bytes 6733828

commit v3 on v2

--- a/solution.py
+++ b/solution.py
@@ -394,7 +394,7 @@
             dma((7,)),
         ],
         compiler_params=pltpu.CompilerParams(
-            collective_id=0, has_side_effects=True, vmem_limit_bytes=40 * 1024 * 1024
+            collective_id=0, has_side_effects=True, vmem_limit_bytes=67043328
         ),
     )(flat, band_counts, dep_blocks, lon_entry, lon_offset, lon_frac, lat_offset, lat_frac)
     moved = jnp.where(lax.axis_index("tm") > 0, prev.astype(jnp.float32), 0.0)

time: 61.3 us -> 56.5 us (0.922)
  local copies, waits for them, and re-layouts: 7.25 us -> 1.37 us
  Pallas kernels: 49 us -> 49.8 us
  other arithmetic: 3.65 us -> 4.33 us
    unnamed x17 -> x1, local copies, waits for them, and re-layouts: 7.25 us -> 1.37 us
    pallas_call x1, Pallas kernels: 49 us -> 49.8 us  [body(): pl.pallas_call(functools.partial(kernel, plan, steps, depth, sizes), out_...]
    convert_element_type x1, other arithmetic: 3.65 us -> 4.33 us  [body(): misfit = (flat.astype(jnp.float32) - moved).astype(state.dtype)]
where the time goes in v3:
time: 56.5 us; the launch traced here: 56.2 us
  Pallas kernels  49.8 us (88%)
  other arithmetic  4.33 us (8%)
  local copies, waits for them, and re-layouts  1.37 us (2%)
  between operations  0.67 us (1%)
    pallas_call x1, Pallas kernels, body(): pl.pallas_call(functools.partial(kernel, plan, steps, depth, sizes), out_...  49.8 us
    convert_element_type x1, other arithmetic, body(): misfit = (flat.astype(jnp.float32) - moved).astype(state.dtype)  4.33 us
    unnamed x1, local copies, waits for them, and re-layouts  1.37 us

profile of v3, /device:TPU:1, one launch (start us, length us, event | category | flops | bytes accessed | tf_op | source)
XLA Modules:
  0.0 56.2 jit_solution(17618451677227850908)
XLA Ops:
  0.0 1.4 %copy.9.lists = s32[1,8,2,6]{3,2,1,0:T(2,128)} copy(s32[1,8,2,6]{1,2,3,0:T(2,128)} %param.10) | data formatting | bytes 768 | tf_op args[2]
  2.0 49.8 %shard_map.82 = bf16[548,8,256]{2,1,0:T(8,128)(2,1)} custom-call(bf16[548,8,256]{2,1,0:T(8,128)(2,1)} %bitcast.3, s32[1,1]{1,0:T(1,128)S(6)} %copy.10.counts, s32[1,8,2,6]{3,2,1,0:T(2,128)} %copy.9.lists, s32[1,8,256]{2,1,0:T(8,128)} %rest_refs_0_.1, s32[1,8,256]{2,1,0:T(8,128)} %rest_refs_1_.1, f32[1,8,256]{2,1,0:T(8,128)} %rest_refs_2_.1, ...), custom_call_target="tpu_custom_call" | custom-call | tf_op jit(solution)/shard_map/pallas_call | solution.py:364
  51.9 4.3 %subtract_convert_fusion = bf16[548,8,256]{2,1,0:T(8,128)(2,1)} fusion(bf16[548,8,256]{2,1,0:T(8,128)(2,1)} %shard_map.82, pred[]{:T(512)S(6)} %gt.3, bf16[1,4,137,8,256]{4,3,2,1,0:T(8,128)(2,1)} %param.8), kind=kLoop, calls=%fused_computation | loop fusion | flops 5611520 | bytes 6733825 | tf_op jit(solution)/shard_map/convert_element_type | solution.py:401

commit v4 on v3

--- a/solution.py
+++ b/solution.py
@@ -105,13 +105,14 @@
             device_id={"tm": helper}, device_id_type=MESH,
         )
 
-    def x_copies(c, short):
+    def x_copies(c, short, source=None):
+        source = own.at[c] if source is None else source
         part = pl.ds(CHUNK - rest, rest) if short else pl.ds(0, CHUNK)
         copies = []
         for i, (offset, block, number, _) in enumerate(pieces):
             copies.append(
                 pltpu.make_async_remote_copy(
-                    src_ref=own.at[c, part, :, pl.ds(block * BLK, number * BLK)],
+                    src_ref=source.at[part, :, pl.ds(block * BLK, number * BLK)],
                     dst_ref=remotes[i].at[c, part],
                     send_sem=x_send.at[i, c], recv_sem=x_recv.at[i, c],
                     device_id={"lon": lax.rem(lon - offset + 2 * n_lon, n_lon)},
@@ -120,15 +121,15 @@
             )
         return copies
 
-    def each_x(c, act):
+    def each_x(c, act, source=None):
         @pl.when(c < steps - 1)
         def _():
-            for copy in x_copies(c, False):
+            for copy in x_copies(c, False, source):
                 act(copy)
 
         @pl.when(c == steps - 1)
         def _():
-            for copy in x_copies(c, True):
+            for copy in x_copies(c, True, source):
                 act(copy)
 
     def halo_up(c):
@@ -178,7 +179,12 @@
 
     @pl.when(local)
     def _():
+        def send(c):
+            each_x(c, lambda copy: copy.start(), state.at[pl.ds(begin(c), CHUNK)])
+
+        loop(first, jnp.minimum(first + 1, last), send)
         loop(first, last, lambda c: own_copy(c).start())
+        loop(jnp.minimum(first + 1, last), last, send)
         for copy in aux:
             copy.start()
 
@@ -192,8 +198,11 @@
         own_copy(c).wait()
         each_x(c, lambda copy: copy.start())
 
-    ahead = jnp.where(is_helper, 2, steps)
-    loop(first, jnp.minimum(first + ahead, last), forward)
+    ahead = 2
+
+    @pl.when(is_helper)
+    def _():
+        loop(first, jnp.minimum(first + ahead, last), forward)
 
     @pl.when(lat == 0)
     def _():
@@ -207,7 +216,7 @@
         for copy in aux:
             copy.wait()
         entry, offset, lon_fraction, lat_shift, lat_fraction = [v[...] for v in arrays_v]
-        per_list = lists.shape[-1]
+        per_list = lists.shape[1]
         for _ in range((per_list - 1) // 2):
             entry = jnp.where(entry >= counts_s[0, 0], entry - counts_s[0, 0], entry)
         blocks = cols // BLK
@@ -217,7 +226,7 @@
                 wanted = entry[r : r + 1, g * BLK : (g + 1) * BLK]
                 chosen = jnp.zeros((1, BLK), jnp.int32)
                 for k in range(per_list):
-                    q = lists_s[0, r, g, k] - lon * blocks + blocks + blocks // 2 + total
+                    q = lists_s[0, k, g, r] - lon * blocks + blocks + blocks // 2 + total
                     q = lax.rem(q, total)
                     slot = jnp.int32(slots[0])
                     for i in range(1, len(slots)):
@@ -249,6 +258,10 @@
             )
 
     def advect(c):
+        @pl.when(local)
+        def _():
+            own_copy(c).wait()
+
         each_x(c, lambda copy: copy.wait_recv())
         at = 0
         for buffer in (own, *remotes):
@@ -265,38 +278,45 @@
                 jnp.concatenate(parts, axis=1), matrix[r], preferred_element_type=jnp.float32
             )
             adv[c, r + 2] = total.astype(adv.dtype)
-
-        @pl.when(lat < n_lat - 1)
-        def _():
-            halo_up(c).start()
-
-        @pl.when(lat > 0)
-        def _():
-            halo_down(c).start()
+            if r == 2:
+
+                @pl.when(lat < n_lat - 1)
+                def _():
+                    halo_up(c).start()
+
+                @pl.when(lat > 0)
+                def _():
+                    halo_down(c).start()
 
     def finish(c):
-        @pl.when(lat > 0)
-        def _():
-            halo_up(c).wait_recv()
-
-        @pl.when(lat < n_lat - 1)
-        def _():
-            halo_down(c).wait_recv()
-
-        for r in range(rows):
+        def interpolate(r):
             total = None
             for shift in range(5):
                 term = params[6 + shift, r : r + 1, :] * adv[c, r + shift].astype(jnp.float32)
                 total = term if total is None else total + term
             for b in range(cols // BLK):
                 f_end[b, pl.ds(r, CHUNK, stride=rows), :] = total[:, b * BLK : (b + 1) * BLK]
+
+        for r in range(2, rows - 2):
+            interpolate(r)
+
+        @pl.when(lat > 0)
+        def _():
+            halo_up(c).wait_recv()
+
+        @pl.when(lat < n_lat - 1)
+        def _():
+            halo_down(c).wait_recv()
+
+        for r in (0, 1, rows - 2, rows - 1):
+            interpolate(r)
         for b in range(cols // BLK):
             part = f_end[b].reshape(CHUNK, rows, BLK).astype(ends.dtype)
             ends[c, :, :, b * BLK : (b + 1) * BLK] = part
         each_end(c, lambda copy: copy.start())
 
     def step(c):
-        @pl.when(c + ahead < last)
+        @pl.when(jnp.logical_and(is_helper, c + ahead < last))
         def _():
             forward(c + ahead)
 
@@ -359,18 +379,19 @@
     steps = -(-depth // CHUNK)
     flat = state.reshape(depth, rows, cols)
 
+    lists = jnp.transpose(dep_blocks, (0, 3, 2, 1))
     dma = pltpu.SemaphoreType.DMA
     n_pieces = len(pieces)
     prev = pl.pallas_call(
         functools.partial(kernel, plan, steps, depth, sizes),
-        out_shape=jax.ShapeDtypeStruct(flat.shape, flat.dtype),
+        out_shape=pltpu.VMEM(flat.shape, flat.dtype),
         in_specs=[pl.BlockSpec(memory_space=pltpu.HBM)] * 8,
         out_specs=pl.BlockSpec(memory_space=pl.ANY),
         scratch_shapes=[
             pltpu.VMEM((steps, CHUNK, rows, cols), flat.dtype),
             *[pltpu.VMEM((steps, CHUNK, rows, p[2] * BLK), flat.dtype) for p in pieces],
             pltpu.SMEM(band_counts.shape, jnp.int32),
-            pltpu.SMEM(dep_blocks.shape, jnp.int32),
+            pltpu.SMEM(lists.shape, jnp.int32),
             *[
                 pltpu.VMEM((rows, cols), kind.dtype)
                 for kind in (lon_entry, lon_offset, lon_frac, lat_offset, lat_frac)
@@ -394,9 +415,16 @@
             dma((7,)),
         ],
         compiler_params=pltpu.CompilerParams(
-            collective_id=0, has_side_effects=True, vmem_limit_bytes=67043328
+            collective_id=0, has_side_effects=True, vmem_limit_bytes=60 * 1024 * 1024
         ),
-    )(flat, band_counts, dep_blocks, lon_entry, lon_offset, lon_frac, lat_offset, lat_frac)
+    )(
+        pltpu.with_memory_space_constraint(flat, pltpu.HBM),
+        band_counts,
+        *[
+            pltpu.with_memory_space_constraint(array, pltpu.HBM)
+            for array in (lists, lon_entry, lon_offset, lon_frac, lat_offset, lat_frac)
+        ],
+    )
     moved = jnp.where(lax.axis_index("tm") > 0, prev.astype(jnp.float32), 0.0)
     misfit = (flat.astype(jnp.float32) - moved).astype(state.dtype)
     return misfit.reshape(state.shape)

time: 56.5 us -> 53.3 us (0.943)
  local copies, waits for them, and re-layouts: 1.37 us -> 0 us
  Pallas kernels: 49.8 us -> 48.6 us
  other arithmetic: 4.33 us -> 3.66 us
    unnamed x1 -> x0, local copies, waits for them, and re-layouts: 1.37 us -> none
    pallas_call x1, Pallas kernels: 49.8 us -> 48.6 us  [body(): pl.pallas_call(functools.partial(kernel, plan, steps, depth, sizes), out_...]
    convert_element_type x1, other arithmetic: 4.33 us -> 3.66 us  [body(): misfit = (flat.astype(jnp.float32) - moved).astype(state.dtype)]
where the time goes in v4:
time: 53.3 us; the launch traced here: 53 us
  Pallas kernels  48.6 us (91%)
  other arithmetic  3.66 us (7%)
  between operations  0.66 us (1%)
    pallas_call x1, Pallas kernels, body(): pl.pallas_call(functools.partial(kernel, plan, steps, depth, sizes), out_...  48.6 us
    convert_element_type x1, other arithmetic, body(): misfit = (flat.astype(jnp.float32) - moved).astype(state.dtype)  3.66 us

profile of v4, /device:TPU:1, one launch (start us, length us, event | category | flops | bytes accessed | tf_op | source)
XLA Modules:
  0.0 53.0 jit_solution(15665555159612372709)
XLA Ops:
  0.7 48.6 %shard_map.82 = bf16[548,8,256]{2,1,0:T(8,128)(2,1)S(1)} custom-call(bf16[548,8,256]{2,1,0:T(8,128)(2,1)} %bitcast.4, s32[1,1]{1,0:T(1,128)S(6)} %copy.9.counts, s32[1,6,2,8]{3,2,1,0:T(2,128)} %bitcast.5, s32[1,8,256]{2,1,0:T(8,128)} %rest_refs_0_.1, s32[1,8,256]{2,1,0:T(8,128)} %rest_refs_1_.1, f32[1,8,256]{2,1,0:T(8,128)} %rest_refs_2_.1, ...), custom_call_target="tpu_custom_call" | custom-call | tf_op jit(solution)/shard_map/pallas_call | solution.py:385
  49.3 3.7 %subtract_convert_fusion = bf16[548,8,256]{2,1,0:T(8,128)(2,1)} fusion(bf16[548,8,256]{2,1,0:T(8,128)(2,1)S(1)} %shard_map.82, pred[]{:T(512)S(6)} %gt.3, bf16[1,4,137,8,256]{4,3,2,1,0:T(8,128)(2,1)} %param.8), kind=kLoop, calls=%fused_computation | loop fusion | flops 5611520 | bytes 6733825 | tf_op jit(solution)/shard_map/convert_element_type | solution.py:429

commit v5 on v4

--- a/solution.py
+++ b/solution.py
@@ -41,12 +41,12 @@
 
 def kernel(plan, steps, depth, sizes, state, counts, lists, *rest_refs):
     slots, pieces, n_src = plan
-    arrays, prev, scratch = rest_refs[:5], rest_refs[5], rest_refs[6:]
+    arrays, result, scratch = rest_refs[:5], rest_refs[5], rest_refs[6:]
     n_tm, n_lat, n_lon = sizes
     n_pieces = len(pieces)
     own, remotes = scratch[0], scratch[1 : 1 + n_pieces]
     (
-        counts_s, lists_s, *arrays_v, flat, params, matrix, adv, f_end, ends, own_sem, x_send, x_recv,
+        mine, prev, m_sem, counts_s, lists_s, *arrays_v, flat, params, matrix, adv, f_end, ends, own_sem, x_send, x_recv,
         h_send, h_recv, t_send, t_recv, raw_send, p_send, p_recv, a_sem,
     ) = scratch[1 + n_pieces :]
     rows, cols = state.shape[1:]
@@ -197,6 +197,11 @@
     def forward(c):
         own_copy(c).wait()
         each_x(c, lambda copy: copy.start())
+
+    to_mine = pltpu.make_async_copy(state, mine, m_sem)
+    to_result = pltpu.make_async_copy(state, result, m_sem)
+    pl.when(tm > 0)(to_mine.start)
+    pl.when(tm == 0)(to_result.start)
 
     ahead = 2
 
@@ -356,18 +361,31 @@
 
         loop(0, rows, build)
         loop(first, last + 1, step)
-        loop(first, last, settle)
-
+
+    def subtract(place):
+        moved = prev[place].astype(jnp.float32)
+        result[place] = (mine[place].astype(jnp.float32) - moved).astype(result.dtype)
+
+    @pl.when(tm > 0)
+    def _():
+        to_mine.wait()
+
+        def collect(c):
+            end_copy(c, False).wait_recv()
+            subtract(pl.ds(c * CHUNK, CHUNK))
+
+        loop(0, steps - 1, collect)
+        end_copy(steps - 1, True).wait_recv()
+        subtract(pl.ds((steps - 1) * CHUNK, rest))
+
+    pl.when(tm == 0)(to_result.wait)
+    loop(first, last, settle)
     if helping:
 
         @pl.when(tm == helped)
         def _():
             prm_copy().wait_send()
             loop(half, steps, lambda c: raw_copy(c).wait_send())
-
-    @pl.when(tm > 0)
-    def _():
-        loop(0, steps, lambda c: each_end(c, lambda copy: copy.wait_recv()))
 
 
 def body(sizes, state, band_counts, dep_blocks, lon_entry, lon_offset, lon_frac, lat_offset, lat_frac):
@@ -382,14 +400,17 @@
     lists = jnp.transpose(dep_blocks, (0, 3, 2, 1))
     dma = pltpu.SemaphoreType.DMA
     n_pieces = len(pieces)
-    prev = pl.pallas_call(
+    misfit = pl.pallas_call(
         functools.partial(kernel, plan, steps, depth, sizes),
         out_shape=pltpu.VMEM(flat.shape, flat.dtype),
         in_specs=[pl.BlockSpec(memory_space=pltpu.HBM)] * 8,
-        out_specs=pl.BlockSpec(memory_space=pl.ANY),
+        out_specs=pl.BlockSpec(memory_space=pltpu.VMEM),
         scratch_shapes=[
             pltpu.VMEM((steps, CHUNK, rows, cols), flat.dtype),
             *[pltpu.VMEM((steps, CHUNK, rows, p[2] * BLK), flat.dtype) for p in pieces],
+            pltpu.VMEM(flat.shape, flat.dtype),
+            pltpu.VMEM(flat.shape, flat.dtype),
+            dma(()),
             pltpu.SMEM(band_counts.shape, jnp.int32),
             pltpu.SMEM(lists.shape, jnp.int32),
             *[
@@ -425,8 +446,6 @@
             for array in (lists, lon_entry, lon_offset, lon_frac, lat_offset, lat_frac)
         ],
     )
-    moved = jnp.where(lax.axis_index("tm") > 0, prev.astype(jnp.float32), 0.0)
-    misfit = (flat.astype(jnp.float32) - moved).astype(state.dtype)
     return misfit.reshape(state.shape)
 
 

time: 53.3 us -> 51 us (0.957)
  other arithmetic: 3.66 us -> 0 us
  local copies, waits for them, and re-layouts: 0 us -> 1.37 us
    convert_element_type x1 -> x0, other arithmetic: 3.66 us -> none  [body(): misfit = (flat.astype(jnp.float32) - moved).astype(state.dtype)]
    unnamed x0 -> x1, local copies, waits for them, and re-layouts: none -> 1.37 us
where the time goes in v5:
time: 51 us; the launch traced here: 50.8 us
  Pallas kernels  48.8 us (96%)
  local copies, waits for them, and re-layouts  1.37 us (3%)
  between operations  0.66 us (1%)
    pallas_call x1, Pallas kernels, body(): pl.pallas_call(functools.partial(kernel, plan, steps, depth, sizes), out_...  48.8 us
    unnamed x1, local copies, waits for them, and re-layouts  1.37 us

profile of v5, /device:TPU:1, one launch (start us, length us, event | category | flops | bytes accessed | tf_op | source)
XLA Modules:
  0.0 50.8 jit_solution(10589540007255943355)
XLA Ops:
  0.7 48.8 %shard_map.82 = bf16[548,8,256]{2,1,0:T(8,128)(2,1)S(1)} custom-call(bf16[548,8,256]{2,1,0:T(8,128)(2,1)} %bitcast.4, s32[1,1]{1,0:T(1,128)S(6)} %copy.11.counts, s32[1,6,2,8]{3,2,1,0:T(2,128)} %bitcast.5, s32[1,8,256]{2,1,0:T(8,128)} %rest_refs_0_.1, s32[1,8,256]{2,1,0:T(8,128)} %rest_refs_1_.1, f32[1,8,256]{2,1,0:T(8,128)} %rest_refs_2_.1, ...), custom_call_target="tpu_custom_call" | custom-call | tf_op jit(solution)/shard_map/pallas_call | solution.py:403
  49.4 1.4 %copy.10 = bf16[1,4,137,8,256]{4,3,2,1,0:T(8,128)(2,1)} copy(bf16[1,4,137,8,256]{4,3,2,1,0:T(8,128)(2,1)S(1)} %bitcast.3) | data formatting | bytes 4489216

commit v6 on v5

--- a/solution.py
+++ b/solution.py
@@ -8,7 +8,7 @@
 from jax.sharding import PartitionSpec as P
 
 BLK = 128
-CHUNK = 72
+CHUNK = 56
 MESH = pl.DeviceIdType.MESH
 
 

time: 51 us -> 50.5 us (level)
  no operation moved by 1% of the time
where the time goes in v6:
time: 50.5 us; the launch traced here: 50.4 us
  Pallas kernels  48.4 us (96%)
  local copies, waits for them, and re-layouts  1.37 us (3%)
  between operations  0.66 us (1%)
    pallas_call x1, Pallas kernels, body(): pl.pallas_call(functools.partial(kernel, plan, steps, depth, sizes), out_...  48.4 us
    unnamed x1, local copies, waits for them, and re-layouts  1.37 us

profile of v6, /device:TPU:1, one launch (start us, length us, event | category | flops | bytes accessed | tf_op | source)
XLA Modules:
  0.0 50.4 jit_solution(3206501992335393417)
XLA Ops:
  0.7 48.4 %shard_map.82 = bf16[548,8,256]{2,1,0:T(8,128)(2,1)S(1)} custom-call(bf16[548,8,256]{2,1,0:T(8,128)(2,1)} %bitcast.4, s32[1,1]{1,0:T(1,128)S(6)} %copy.11.counts, s32[1,6,2,8]{3,2,1,0:T(2,128)} %bitcast.5, s32[1,8,256]{2,1,0:T(8,128)} %rest_refs_0_.1, s32[1,8,256]{2,1,0:T(8,128)} %rest_refs_1_.1, f32[1,8,256]{2,1,0:T(8,128)} %rest_refs_2_.1, ...), custom_call_target="tpu_custom_call" | custom-call | tf_op jit(solution)/shard_map/pallas_call | solution.py:403
  49.0 1.4 %copy.10 = bf16[1,4,137,8,256]{4,3,2,1,0:T(8,128)(2,1)} copy(bf16[1,4,137,8,256]{4,3,2,1,0:T(8,128)(2,1)S(1)} %bitcast.3) | data formatting | bytes 4489216
